TPU v7x, 32 devices: a whole 2x2x4 slice. The times are simulated.
32 devices in a mesh: groups: 2 (over y), seq: 4 (over z), dp: 4 (over x, core), head: 1.
Axes of the slice: x: 2, y: 2, z: 4, core: 2. Of those that a mesh axis runs over, the one named last changes fastest.
Arguments:
- x_in: bfloat16 [8, 2048, 768], P(('groups', 'dp'), 'seq'), parts along dimension 0, may hold values from -6 to 6
- kernel_weight: bfloat16 [3, 768, 1536], P(None, None, 'head'), may hold values from -0.125 to 0.125
- conv_bias: float32 [1536], P('head'), may hold values from -3 to 3
- norm_gain: float32 [1536], replicated, may hold values from 0.25 to 1.75
- w_query: bfloat16 [1536, 1024], P(None, 'head'), may hold values from -8 to 8
- w_key: bfloat16 [1536, 128], replicated, may hold values from -1 to 1
- w_value: bfloat16 [1536, 192], replicated, may hold values from -0.15625 to 0.15625
- w_out: bfloat16 [1536, 1536], P('head'), may hold values from -0.15625 to 0.15625
- cotangent: bfloat16 [8, 1024, 1536], P(('groups', 'dp'), 'seq'), parts along dimension 0, may hold values from -0.75 to 0.75
Outputs:
- mixed: bfloat16 [8, 1024, 1536], P(('groups', 'dp'), 'seq', 'head'), parts along dimension 0
- grad_out_t: float32 [3072, 1536], P(('groups', 'dp'), 'head'), parts along dimension 0
There are 2 independent parts, one for each index of `groups`. A program takes and returns all parts, laid end to end along the dimension named above; an argument that names none is the same for every part. Nothing has to cross between parts.
All inputs are finite; a program needn't handle non-finite values.
Results may differ from a plain program's by a relative error of at most 0.02.
Values may be sent and summed in bfloat16 or wider, within the bound.
A program may use at most 128 MiB of HBM per device.

v0:
```python
import math
import jax
import jax.numpy as jnp
from jax import lax
from jax.sharding import PartitionSpec as P

KEY = 128
VAL = 192
KERNEL_TAPS = 3
DILATION_STEP = 2
rope_base = 10000.0
norm_eps = 1e-06


def padded(cells, sides, width):
    for axis, dim in sides:
        count = lax.axis_size(axis)
        ends = count - 1
        head = lax.slice_in_dim(cells, 0, width, axis=dim)
        tail = lax.slice_in_dim(cells, cells.shape[dim] - width, cells.shape[dim], axis=dim)
        cells = jnp.concatenate(
            [
                lax.ppermute(tail, axis, [(i, (i + 1) % count) for i in range(ends)]),
                cells,
                lax.ppermute(head, axis, [((i + 1) % count, i) for i in range(ends)]),
            ],
            axis=dim,
        )
    return cells


def rotate(vectors, positions):
    halfway = vectors.shape[-1] // 2
    frequency = jnp.exp(
        -math.log(rope_base) * 2.0 * jnp.arange(halfway, dtype=jnp.float32) / vectors.shape[-1]
    )
    angles = positions.astype(jnp.float32)[:, None] * frequency[None, :]
    layout = (positions.shape[0],) + (1,) * (vectors.ndim - 2) + (halfway,)
    cosine = jnp.cos(angles).reshape(layout)
    sines = jnp.sin(angles).reshape(layout)
    leading = vectors[..., :halfway]
    trailing = vectors[..., halfway:]
    return jnp.concatenate(
        [leading * cosine - trailing * sines, leading * sines + trailing * cosine], axis=-1
    )


def attend_pieces(queries, key_rows, value_rows, state_in):
    total_keys = key_rows.shape[0]
    block_size = math.gcd(total_keys, 512)

    def one_block(block_index, state):
        running_max, running_sum, weighted = state
        key_block = lax.dynamic_slice_in_dim(key_rows, block_index * block_size, block_size, 0)
        value_block = lax.dynamic_slice_in_dim(value_rows, block_index * block_size, block_size, 0)
        scores = jnp.einsum(
            "thd,ud->htu", queries, key_block, preferred_element_type=jnp.float32
        ) * KEY ** (-0.5)
        new_max = jnp.maximum(running_max, jnp.max(scores, axis=-1))
        rescale = jnp.exp(running_max - new_max)
        weights = jnp.exp(scores - new_max[:, :, None])
        running_sum = running_sum * rescale + jnp.sum(weights, axis=-1)
        weighted = weighted * jnp.transpose(rescale)[:, :, None] + jnp.einsum(
            "htu,uv->thv",
            weights.astype(jnp.bfloat16),
            value_block,
            preferred_element_type=jnp.float32,
        )
        return (new_max, running_sum, weighted)

    return lax.fori_loop(0, total_keys // block_size, one_block, state_in)


def local(x_in, kernel_weight, conv_bias, norm_gain, w_query, w_key, w_value, w_out, cotangent):
    inputs = x_in[0]
    edge_padding = DILATION_STEP * (KERNEL_TAPS - 1) // 2
    padded_rows = padded(inputs, (("seq", 0),), edge_padding)
    padded_row_count = inputs.shape[0]
    before_activation = jnp.broadcast_to(
        conv_bias[None, :], (padded_row_count, kernel_weight.shape[2])
    )
    for kernel_tap_index in range(KERNEL_TAPS):
        before_activation = before_activation + jnp.dot(
            padded_rows[
                kernel_tap_index * DILATION_STEP : kernel_tap_index * DILATION_STEP
                + padded_row_count
            ],
            kernel_weight[kernel_tap_index],
            preferred_element_type=jnp.float32,
        )
    activated = jax.nn.gelu(before_activation)
    pooled = jnp.max(activated.reshape(padded_row_count // 2, 2, -1), axis=1).astype(jnp.bfloat16)
    token_count = pooled.shape[0]
    features = lax.all_gather(pooled, "head", axis=1, tiled=True)
    widened = features.astype(jnp.float32)
    squares = jnp.mean(widened * widened, axis=-1, keepdims=True)
    normed = (widened * lax.rsqrt(squares + norm_eps) * norm_gain).astype(jnp.bfloat16)
    seq_offset = lax.axis_index("seq") * token_count
    positions = seq_offset + jnp.arange(token_count, dtype=jnp.int32)
    local_heads = w_query.shape[1] // KEY
    queries = rotate(
        jnp.dot(normed, w_query, preferred_element_type=jnp.float32).reshape(
            token_count, local_heads, KEY
        ),
        positions,
    ).astype(jnp.bfloat16)
    own_rows = token_count // lax.axis_size("head")
    row_offset = lax.axis_index("head") * own_rows
    own_normed = lax.dynamic_slice_in_dim(normed, row_offset, own_rows, 0)
    own_positions = seq_offset + row_offset + jnp.arange(own_rows, dtype=jnp.int32)
    key_rows = rotate(
        jnp.dot(own_normed, w_key, preferred_element_type=jnp.float32), own_positions
    ).astype(jnp.bfloat16)
    value_rows = jnp.dot(own_normed, w_value, preferred_element_type=jnp.float32).astype(
        jnp.bfloat16
    )
    start_state = (
        jnp.full((local_heads, token_count), -1e30, jnp.float32),
        jnp.zeros((local_heads, token_count), jnp.float32),
        jnp.zeros((token_count, local_heads, VAL), jnp.float32),
    )
    final_state = attend_pieces(
        queries,
        lax.all_gather(key_rows, ("seq", "head"), axis=0, tiled=True),
        lax.all_gather(value_rows, ("seq", "head"), axis=0, tiled=True),
        start_state,
    )
    running_max, running_sum, weighted = final_state
    attended = (
        (weighted / jnp.transpose(running_sum)[:, :, None])
        .astype(jnp.bfloat16)
        .reshape(token_count, local_heads * VAL)
    )
    projected = lax.psum_scatter(
        lax.dot_general(
            w_out, attended, (((0,), (1,)), ((), ())), preferred_element_type=jnp.float32
        ).astype(jnp.bfloat16),
        "head",
        scatter_dimension=0,
        tiled=True,
    ).astype(jnp.float32)
    mixed = (pooled.astype(jnp.float32) + jnp.transpose(projected)).astype(jnp.bfloat16)[None]
    upstream = cotangent[0]
    dp_rows = upstream.shape[1] // lax.axis_size("dp")
    whole_grad = lax.dot_general(
        upstream, attended, (((0,), (0,)), ((), ())), preferred_element_type=jnp.float32
    )
    summed = lax.psum(whole_grad, ("seq", "dp"))
    gradient = lax.dynamic_slice_in_dim(summed, lax.axis_index("dp") * dp_rows, dp_rows, 0)
    return (mixed, gradient)


def solution(mesh):
    return jax.shard_map(
        local,
        mesh=mesh,
        in_specs=(
            P(("groups", "dp"), "seq", None),
            P(None, None, "head"),
            P("head"),
            P(),
            P(None, "head"),
            P(),
            P(),
            P("head", None),
            P(("groups", "dp"), "seq", None),
        ),
        out_specs=(P(("groups", "dp"), "seq", "head"), P(("groups", "dp"), "head")),
        check_vma=False,
    )
```

profile of v0, /device:TPU:0, one launch (start us, length us, event | category | flops | bytes accessed | tf_op | source)
XLA Modules:
  0.0 299.3 jit_solution(1337052279311216444)
XLA Ops:
  8.1 1.4 collective-permute-start.1
  9.5 5.6 %collective-permute-start = (bf16[2,768]{1,0:T(2,128)(2,1)S(1)}, bf16[2,768]{1,0:T(2,128)(2,1)S(1)}, u32[]{:S(2)}, u32[]{:S(2)}) collective-permute-start(bf16[2,768]{1,0:T(2,128)(2,1)S(1)} %get-tuple-element.185), channel_id=1, source_target_pairs={{0,4},{4,8},{8,12},{1,5},{5,9},{9,13},{2,6},{6,10},{10,14},{3,7},{... | collective-permute-start | bytes 9224 | tf_op jit(solution)/shard_map/ppermute | solution.py:23
  15.1 5.0 %fusion.32 = f32[512,1536]{1,0:T(8,128)} fusion(bf16[3,768,1536]{2,1,0:T(8,128)(2,1)} %param.12, bf16[1,512,768]{2,1,0:T(8,128)(2,1)} %param.11), kind=kOutput, calls=%fused_computation.43 | convolution fusion | flops 1207959552 | bytes 6291456 | tf_op jit(solution)/shard_map/dot_general | solution.py:83
  20.1 4.3 %fusion.19 = f32[512,1536]{1,0:T(8,128)S(1)} fusion(f32[512,1536]{1,0:T(8,128)} %fusion.32, bf16[3,768,1536]{2,1,0:T(8,128)(2,1)} %param.12, f32[1536]{0:T(1024)S(1)} %copy-done.8, bf16[512,768]{1,0:T(8,128)(2,1)} %bitcast.80, bf16[2,768]{1,0:T(2,128)(2,1)S(1)} %collective-permute-done), kind=kOutput, calls=%fused_computation.27 | convolution fusion | flops 1211105280 | bytes 9446400 | tf_op jit(solution)/shard_map/dot_general | solution.py:83
  24.5 4.8 %fusion.26 = bf16[512,1536]{1,0:T(8,128)(2,1)} fusion(f32[512,1536]{1,0:T(8,128)S(1)} %fusion.19, bf16[3,768,1536]{2,1,0:T(8,128)(2,1)} %param.12, bf16[2,768]{1,0:T(2,128)(2,1)S(1)} %collective-permute-done.1, bf16[512,768]{1,0:T(8,128)(2,1)S(1)} %bitcast.81), kind=kOutput, calls=%fused_computation.34 | convolution fusion | flops 1217396736 | bytes 7867392 | tf_op jit(solution)/shard_map/dot_general | solution.py:83
  29.3 4.5 %reshape.92 = bf16[256,2,1536]{2,1,0:T(2,128)(2,1)} reshape(bf16[512,1536]{1,0:T(8,128)(2,1)} %fusion.26) | data formatting | bytes 3145728 | tf_op jit(solution)/shard_map/reshape | solution.py:92
  33.8 6.1 %reduce_max.22 = bf16[256,1536]{1,0:T(8,128)(2,1)} reduce(bf16[256,2,1536]{2,1,0:T(2,128)(2,1)} %reshape.92, bf16[]{:T(256)} %constant.148), dimensions={1}, to_apply=%region_0.0 | reduce | flops 393216 | bytes 2359298 | tf_op jit(solution)/shard_map/reduce_max | solution.py:92
  39.9 1.4 fusion.38
  41.3 2.4 convolution_convert_fusion.1
  43.7 1.7 fusion.50
  47.3 15.7 %all_gather.7 = bf16[1024,128]{0,1:T(8,128)(2,1)} all-gather(bf16[256,128]{0,1:T(8,128)(2,1)S(1)} %pad_maximum_fusion.5), channel_id=1, replica_groups=mesh['groups'=2,'seq'=4,'dp'=4,'head'=1] {'seq','head'}, dimensions={0}, use_global_device_ids=true | all-gather | bytes 327680 | tf_op jit(solution)/shard_map/all_gather | solution.py:124
  63.0 15.1 %all_gather.8 = bf16[1024,192]{0,1:T(8,128)(2,1)S(1)} all-gather(bf16[256,192]{0,1:T(8,128)(2,1)} %convolution_convert_fusion.1), channel_id=1, replica_groups=mesh['groups'=2,'seq'=4,'dp'=4,'head'=1] {'seq','head'}, dimensions={0}, use_global_device_ids=true | all-gather | bytes 491520 | tf_op jit(solution)/shard_map/all_gather | solution.py:125
  78.1 2.2 convolution_bitcast_fusion.1
  82.8 11.4 %while.18 = (s32[]{:T(128)}, f32[8,256]{1,0:T(8,128)S(1)}, f32[8,256]{1,0:T(8,128)S(1)}, f32[256,8,192]{0,2,1:T(8,128)}, bf16[1024,128]{0,1:T(8,128)(2,1)}, /*in...) while((s32[]{:T(128)}, f32[8,256]{1,0:T(8,128)S(1)}, ...), condition=%wide.region_5.0_spmd.clone, body=%wide.region_2.0_spmd.clone.sunk | while | flops 680669184 | bytes 29294832 | solution.py:71
  82.8 1.9 bitcast_reduce_fusion.2
  86.1 1.3 bitcast_add_fusion.2
  88.5 1.9 bitcast_reduce_fusion.2
  91.8 1.3 bitcast_add_fusion.2
  94.2 1.5 divide_convert_fusion
  96.6 6.2 %convolution_bitcast_fusion = f32[1536,1536]{0,1:T(8,128)} fusion(bf16[256,1536]{0,1:T(8,128)(2,1)S(1)} %bitcast.77, bf16[1,256,1536]{2,1,0:T(8,128)(2,1)} %param.19), kind=kOutput, calls=%fused_computation.23 | convolution fusion | flops 1207959552 | bytes 11010048 | tf_op jit(solution)/shard_map/dot_general | solution.py:145
  102.8 5.1 %fusion.30 = bf16[1,256,1536]{2,1,0:T(8,128)(2,1)} fusion(bf16[256,1536]{0,1:T(8,128)(2,1)} %bitcast.78, bf16[1536,1536]{1,0:T(8,128)(2,1)} %param.18, bf16[256,1536]{1,0:T(8,128)(2,1)} %reduce_max.22), kind=kOutput, calls=%fused_computation.39 | convolution fusion | flops 1209925632 | bytes 7077888 | tf_op jit(solution)/shard_map/dot_general | solution.py:135
  107.9 178.3 %all-reduce.2.cloned.1.call-done = f32[1536,1536]{0,1:T(8,128)} async-done(((f32[1536,1536]{0,1:T(8,128)}), f32[1536,1536]{0,1:T(8,128)}) %all-reduce.2.cloned.1.call-update) | async-done | bytes 9437200 | tf_op jit(solution)/shard_map/psum | solution.py:148
  286.2 3.2 %constant_dynamic-slice_fusion = f32[384,1536]{0,1:T(8,128)} fusion(f32[1536,1536]{0,1:T(8,128)} %all-reduce.2.cloned.1.call-done, s32[]{:T(128)S(6)} %select_n.12), kind=kLoop, calls=%fused_computation.73 | loop fusion | bytes 4718596 | tf_op jit(solution)/shard_map/dynamic_slice | solution.py:149
  289.4 3.0 %copy.17 = f32[384,1536]{1,0:T(8,128)} copy(f32[384,1536]{0,1:T(8,128)} %constant_dynamic-slice_fusion) | data formatting | bytes 4718592
  (51 shorter events, 11.2 us)
Async XLA Ops:
  7.2 71.0 %copy-start = (bf16[1536,1024]{1,0:T(8,128)(2,1)S(1)}, bf16[1536,1024]{1,0:T(8,128)(2,1)}, u32[]{:S(2)}) copy-start(bf16[1536,1024]{1,0:T(8,128)(2,1)} %param.15) | copy-start | bytes 9437188
  7.2 279.1 %all-reduce.2.cloned.1.call-start = ((), (), s32[]{:S(2)}) async-start(), calls=%async_computation | async-start | bytes 18874368 | tf_op jit(solution)/shard_map/psum | solution.py:148
  8.1 16.3 %collective-permute-start.1 = (bf16[2,768]{1,0:T(2,128)(2,1)S(1)}, bf16[2,768]{1,0:T(2,128)(2,1)S(1)}, u32[]{:S(2)}, u32[]{:S(2)}) collective-permute-start(bf16[2,768]{1,0:T(2,128)(2,1)S(1)} %get-tuple-element.184), channel_id=1, source_target_pairs={{4,0},{8,4},{12,8},{5,1},{9,5},{13,9},{6,2},{10,6},{14,10},{7,3},{... | collective-permute-start | bytes 9224 | tf_op jit(solution)/shard_map/ppermute | solution.py:25
  9.5 10.6 %collective-permute-start = (bf16[2,768]{1,0:T(2,128)(2,1)S(1)}, bf16[2,768]{1,0:T(2,128)(2,1)S(1)}, u32[]{:S(2)}, u32[]{:S(2)}) collective-permute-start(bf16[2,768]{1,0:T(2,128)(2,1)S(1)} %get-tuple-element.185), channel_id=1, source_target_pairs={{0,4},{4,8},{8,12},{1,5},{5,9},{9,13},{2,6},{6,10},{10,14},{3,7},{... | collective-permute-start | bytes 9224 | tf_op jit(solution)/shard_map/ppermute | solution.py:23
  15.1 5.0 %copy-start.8 = (f32[1536]{0:T(1024)S(1)}, f32[1536]{0:T(1024)}, u32[]{:S(2)}) copy-start(f32[1536]{0:T(1024)} %param.13) | copy-start | bytes 18436
  20.1 4.3 %copy-start.7 = (bf16[1,512,768]{2,1,0:T(8,128)(2,1)S(1)}, bf16[1,512,768]{2,1,0:T(8,128)(2,1)}, u32[]{:S(2)}) copy-start(bf16[1,512,768]{2,1,0:T(8,128)(2,1)} %param.11) | copy-start | bytes 2359300
  29.3 12.0 %copy-start.9 = (f32[1536]{0:T(1024)S(1)}, f32[1536]{0:T(1024)}, u32[]{:S(2)}) copy-start(f32[1536]{0:T(1024)} %param.14) | copy-start | bytes 18436
  41.3 6.0 %copy-start.6 = (f32[256]{0:T(256)}, f32[256]{0:T(256)S(1)}, u32[]{:S(2)}) copy-start(f32[256]{0:T(256)S(1)} %add_rsqrt_fusion) | copy-start | bytes 3076
  80.3 0.9 copy-start.4
  80.3 1.0 copy-start.5
  84.6 1.4 copy-start.1
  87.3 1.1 copy-start.2
  90.4 1.4 copy-start.1
  93.1 1.1 copy-start.2
  95.7 0.9 copy-start.3
Sparse Core Ops, SparseCore 0:
  102.9 183.2 all-reduce.1
where the time goes:
time: 300 us; the launch traced here: 299 us
  waiting for transfers between devices  178 us (59%)
  matrix products  37.9 us (13%)
  blocking collectives  30.8 us (10%)
  local copies, waits for them, and re-layouts  18.6 us (6%)
  between operations  14.2 us (5%)
  other arithmetic  12.3 us (4%)
  starting transfers between devices  7.01 us (2%)
    psum x1, waiting for transfers between devices, local(): summed = lax.psum(whole_grad, ('seq', 'dp'))  178 us
    all_gather x1, blocking collectives, local(): lax.all_gather(key_rows, ('seq', 'head'), axis=0, tiled=True)  15.7 us
    all_gather x1, blocking collectives, local(): lax.all_gather(value_rows, ('seq', 'head'), axis=0, tiled=True)  15.1 us
    dot_general x3, matrix products, local(): jnp.dot(padded_rows[kernel_tap_index * DILATION_STEP:kernel_tap_index * D...  14.1 us
    dot_general x1, matrix products, local(): lax.dot_general(upstream, attended, (((0,), (0,)), ((), ())), preferred_e...  6.18 us
    reduce_max x1, other arithmetic, local(): jnp.max(activated.reshape(padded_row_count // 2, 2, -1), axis=1)  6.11 us
  transfers between devices with their start and end apart: 3, of which 1 were waited for; matrix products, arithmetic and copies ran while one was open for 5% of the time, Pallas kernels for 0%

commit v1 on v0

--- a/solution.py
+++ b/solution.py
@@ -145,7 +145,7 @@
     whole_grad = lax.dot_general(
         upstream, attended, (((0,), (0,)), ((), ())), preferred_element_type=jnp.float32
     )
-    summed = lax.psum(whole_grad, ("seq", "dp"))
+    summed = lax.psum(lax.psum(whole_grad, "dp"), "seq")
     gradient = lax.dynamic_slice_in_dim(summed, lax.axis_index("dp") * dp_rows, dp_rows, 0)
     return (mixed, gradient)
 

time: 300 us -> 604 us (2.01)
  waiting for transfers between devices: 178 us -> 490 us
    psum x1 -> x2, waiting for transfers between devices: 178 us -> 490 us  [local(): summed = lax.psum(lax.psum(whole_grad, 'dp'), 'seq')]
  transfers between devices with their start and end apart: 3 -> 4, of which waited for: 1 -> 2; matrix products, arithmetic and copies ran while one was open for 5% -> 2% of each run, Pallas kernels for 0% -> 0%
where the time goes in v1:
time: 604 us; the launch traced here: 603 us
  waiting for transfers between devices  490 us (81%)
  matrix products  35.3 us (6%)
  blocking collectives  30.8 us (5%)
  local copies, waits for them, and re-layouts  15.7 us (3%)
  between operations  14.3 us (2%)
  other arithmetic  10.1 us (2%)
  starting transfers between devices  7.05 us (1%)
    psum x2, waiting for transfers between devices, local(): summed = lax.psum(lax.psum(whole_grad, 'dp'), 'seq')  490 us
    all_gather x1, blocking collectives, local(): lax.all_gather(key_rows, ('seq', 'head'), axis=0, tiled=True)  15.7 us
    all_gather x1, blocking collectives, local(): lax.all_gather(value_rows, ('seq', 'head'), axis=0, tiled=True)  15.1 us
    dot_general x3, matrix products, local(): jnp.dot(padded_rows[kernel_tap_index * DILATION_STEP:kernel_tap_index * D...  14.1 us
  transfers between devices with their start and end apart: 4, of which 2 were waited for; matrix products, arithmetic and copies ran while one was open for 2% of the time, Pallas kernels for 0%

profile of v1, /device:TPU:0, one launch (start us, length us, event | category | flops | bytes accessed | tf_op | source)
XLA Modules:
  0.0 603.4 jit_solution(12666457686414594323)
XLA Ops:
  7.2 0.9 slice_bitcast_fusion
  8.1 1.4 collective-permute-start.1
  9.5 5.6 collective-permute-start
  15.1 4.9 fusion.32
  20.1 4.3 fusion.19
  24.5 4.8 fusion.26
  29.3 4.5 reshape.92
  33.8 6.1 %reduce_max.22 = bf16[256,1536]{1,0:T(8,128)(2,1)} reduce(bf16[256,2,1536]{2,1,0:T(2,128)(2,1)} %reshape.92, bf16[]{:T(256)} %constant.148), dimensions={1}, to_apply=%region_0.0 | reduce | flops 393216 | bytes 2359298 | tf_op jit(solution)/shard_map/reduce_max | solution.py:92
  39.9 1.4 fusion.38
  41.3 2.4 convolution_convert_fusion.1
  43.7 1.7 fusion.50
  47.3 15.7 %all_gather.7 = bf16[1024,128]{0,1:T(8,128)(2,1)} all-gather(bf16[256,128]{0,1:T(8,128)(2,1)S(1)} %pad_maximum_fusion.5), channel_id=1, replica_groups=mesh['groups'=2,'seq'=4,'dp'=4,'head'=1] {'seq','head'}, dimensions={0}, use_global_device_ids=true | all-gather | bytes 327680 | tf_op jit(solution)/shard_map/all_gather | solution.py:124
  63.0 15.1 %all_gather.8 = bf16[1024,192]{0,1:T(8,128)(2,1)S(1)} all-gather(bf16[256,192]{0,1:T(8,128)(2,1)} %convolution_convert_fusion.1), channel_id=1, replica_groups=mesh['groups'=2,'seq'=4,'dp'=4,'head'=1] {'seq','head'}, dimensions={0}, use_global_device_ids=true | all-gather | bytes 491520 | tf_op jit(solution)/shard_map/all_gather | solution.py:125
  78.1 2.2 convolution_bitcast_fusion.1
  82.3 5.6 while.18
  83.8 1.3 bitcast_add_fusion.2
  86.6 1.3 bitcast_add_fusion.2
  88.1 6.2 %convolution_bitcast_fusion = f32[1536,1536]{0,1:T(8,128)} fusion(bf16[256,1536]{0,1:T(8,128)(2,1)S(1)} %bitcast.77, bf16[1,256,1536]{2,1,0:T(8,128)(2,1)} %param.19), kind=kOutput, calls=%fused_computation.23 | convolution fusion | flops 1207959552 | bytes 11010048 | tf_op jit(solution)/shard_map/dot_general | solution.py:145
  94.4 168.3 %all-reduce.3.cloned.1.call-done = f32[1536,1536]{0,1:T(8,128)} async-done(((f32[1536,1536]{0,1:T(8,128)}), f32[1536,1536]{0,1:T(8,128)}) %all-reduce.3.cloned.1.call-update) | async-done | bytes 9437200 | tf_op jit(solution)/shard_map/psum | solution.py:148
  262.8 1.1 copy-done.4
  263.9 4.6 fusion.30
  268.5 321.6 %all-reduce.5.cloned.1.call-done = f32[1536,1536]{0,1:T(8,128)} async-done(((f32[1536,1536]{0,1:T(8,128)}), f32[1536,1536]{0,1:T(8,128)}) %all-reduce.5.cloned.1.call-update) | async-done | bytes 9437200 | tf_op jit(solution)/shard_map/psum | solution.py:148
  590.1 3.4 constant_dynamic-slice_fusion
  593.5 3.0 copy.17
  (52 shorter events, 7.1 us)
Async XLA Ops:
  7.2 71.0 %copy-start = (bf16[1536,1024]{1,0:T(8,128)(2,1)S(1)}, bf16[1536,1024]{1,0:T(8,128)(2,1)}, u32[]{:S(2)}) copy-start(bf16[1536,1024]{1,0:T(8,128)(2,1)} %param.15) | copy-start | bytes 9437188
  7.2 255.6 %all-reduce.3.cloned.1.call-start = ((), (), s32[]{:S(2)}) async-start(), calls=%async_computation | async-start | bytes 18874368 | tf_op jit(solution)/shard_map/psum | solution.py:148
  8.1 16.3 %collective-permute-start.1 = (bf16[2,768]{1,0:T(2,128)(2,1)S(1)}, bf16[2,768]{1,0:T(2,128)(2,1)S(1)}, u32[]{:S(2)}, u32[]{:S(2)}) collective-permute-start(bf16[2,768]{1,0:T(2,128)(2,1)S(1)} %get-tuple-element.184), channel_id=1, source_target_pairs={{4,0},{8,4},{12,8},{5,1},{9,5},{13,9},{6,2},{10,6},{14,10},{7,3},{... | collective-permute-start | bytes 9224 | tf_op jit(solution)/shard_map/ppermute | solution.py:25
  9.5 10.6 %collective-permute-start = (bf16[2,768]{1,0:T(2,128)(2,1)S(1)}, bf16[2,768]{1,0:T(2,128)(2,1)S(1)}, u32[]{:S(2)}, u32[]{:S(2)}) collective-permute-start(bf16[2,768]{1,0:T(2,128)(2,1)S(1)} %get-tuple-element.185), channel_id=1, source_target_pairs={{0,4},{4,8},{8,12},{1,5},{5,9},{9,13},{2,6},{6,10},{10,14},{3,7},{... | collective-permute-start | bytes 9224 | tf_op jit(solution)/shard_map/ppermute | solution.py:23
  15.1 5.0 copy-start.9
  20.1 4.3 copy-start.8
  29.3 12.0 %copy-start.10 = (f32[1536]{0:T(1024)S(1)}, f32[1536]{0:T(1024)}, u32[]{:S(2)}) copy-start(f32[1536]{0:T(1024)} %param.14) | copy-start | bytes 18436
  41.3 6.0 copy-start.7
  80.3 0.9 copy-start.5
  80.3 1.0 copy-start.6
  80.9 1.4 copy-start.2
  80.9 1.4 copy-start.3
  94.4 495.7 %all-reduce.5.cloned.1.call-start = ((), (), s32[]{:S(2)}) async-start(), calls=%async_computation.1 | async-start | bytes 18874368 | tf_op jit(solution)/shard_map/psum | solution.py:148
  262.8 1.1 copy-start.4
  590.1 6.4 %copy-start.1 = (bf16[1536,1024]{1,0:T(8,128)(2,1)S(1)}, bf16[1536,1024]{1,0:T(8,128)(2,1)}, u32[]{:S(2)}) copy-start(bf16[1536,1024]{1,0:T(8,128)(2,1)} %param.15) | copy-start | bytes 9437188
Sparse Core Ops, SparseCore 0:
  94.5 168.2 all-reduce.2
  265.2 324.8 all-reduce.4
